TPU v7x, 32 devices: a whole 2x2x4 slice. The times are simulated.
32 devices in a mesh: clip: 8 (over y, x, core), shard: 4 (over z).
Axes of the slice: x: 2, y: 2, z: 4, core: 2. Of those that a mesh axis runs over, the one named last changes fastest.
Arguments:
- tokens: bfloat16 [8, 9216, 768], P('clip', 'shard'), may hold values from -6 to 6
- scales: float32 [8, 6, 9216], P('clip', None, 'shard'), may hold values from 0.1875 to 5
- slot_params: bfloat16 [768, 128], replicated, may hold values from -2 to 2
- expand_weight: bfloat16 [64, 768, 3072], P(('clip', 'shard')), may hold values from -0.21875 to 0.21875
- expand_bias: bfloat16 [64, 3072], P(('clip', 'shard')), may hold values from -4 to 4
- reduce_weight: bfloat16 [64, 3072, 768], P(('clip', 'shard')), may hold values from -0.109375 to 0.109375
- reduce_bias: bfloat16 [64, 768], P(('clip', 'shard')), may hold values from -4 to 4
Outputs:
- mixed: bfloat16 [8, 9216, 768], P('clip', 'shard')
All inputs are finite; a program needn't handle non-finite values.
Results may differ from a plain program's by a relative error of at most 0.012.
The roundings to bfloat16 on the way count: a program that leaves them out, or rounds other values in their place, can miss the bound.
Values may be sent and summed in bfloat16 or wider, within the bound.
A program may use at most 128 MiB of HBM per device.

v0:
```python
import jax
import jax.numpy as jnp
from jax import lax
from jax.sharding import PartitionSpec as P


def expert_apply(slot_inputs, expand_weight, expand_bias, reduce_weight, reduce_bias):
    widened = slot_inputs.astype(jnp.float32)
    normalized = (
        widened * lax.rsqrt(jnp.mean(widened * widened, axis=-1, keepdims=True) + 1e-06)
    ).astype(jnp.bfloat16)
    hidden = jnp.einsum(
        "cisd,idf->cisf", normalized, expand_weight, preferred_element_type=jnp.float32
    )
    hidden = jax.nn.gelu(
        hidden + expand_bias.astype(jnp.float32)[None, :, None, :], approximate=False
    ).astype(jnp.bfloat16)
    output = jnp.einsum("cisf,ifd->cisd", hidden, reduce_weight, preferred_element_type=jnp.float32)
    return (output + reduce_bias.astype(jnp.float32)[None, :, None, :]).astype(jnp.bfloat16)


def local(tokens, scales, slot_params, expand_weight, expand_bias, reduce_weight, reduce_bias):
    clip_count = lax.axis_size("clip")
    shard_count = lax.axis_size("shard")
    quantized = tokens[0]
    token_count, feature_dim = quantized.shape
    block_count = scales.shape[1]
    slot_count = slot_params.shape[1]
    owner_rows = slot_count // (clip_count * shard_count)
    experts_here = expand_weight.shape[0]
    slots_each = owner_rows // experts_here
    features = (
        quantized.reshape(token_count, block_count, feature_dim // block_count).astype(jnp.float32)
        * scales[0].T[:, :, None]
    )
    features = features.reshape(token_count, feature_dim).astype(jnp.bfloat16)
    logits = jnp.dot(features, slot_params, preferred_element_type=jnp.float32)
    row_peak = jnp.max(logits, axis=1, keepdims=True)
    row_weights = jnp.exp(logits - row_peak)
    combine_weight = (row_weights / jnp.sum(row_weights, axis=1, keepdims=True)).astype(
        jnp.bfloat16
    )
    column_peak = lax.pmax(jnp.max(logits, axis=0), "shard")
    column_total = lax.psum(jnp.sum(jnp.exp(logits - column_peak), axis=0), "shard")
    dispatch = (jnp.exp(logits - column_peak) / column_total).astype(jnp.bfloat16)
    partial_value = lax.dot_general(
        dispatch, features, (((0,), (0,)), ((), ())), preferred_element_type=jnp.float32
    )
    arrived = lax.all_to_all(
        partial_value, ("clip", "shard"), split_axis=0, concat_axis=0, tiled=True
    )
    slot_inputs = jnp.sum(
        arrived.reshape(clip_count, shard_count, owner_rows, feature_dim), axis=1
    ).astype(jnp.bfloat16)
    slot_outputs = expert_apply(
        slot_inputs.reshape(clip_count, experts_here, slots_each, feature_dim),
        expand_weight,
        expand_bias,
        reduce_weight,
        reduce_bias,
    )
    gathered = lax.all_gather(
        slot_outputs.reshape(1, clip_count * owner_rows, feature_dim), "shard", axis=0, tiled=True
    )
    returned = lax.all_to_all(gathered, "clip", split_axis=1, concat_axis=0, tiled=True)
    mixed = jnp.dot(
        combine_weight,
        returned.reshape(slot_count, feature_dim),
        preferred_element_type=jnp.float32,
    ).astype(jnp.bfloat16)
    return mixed[None]


def solution(mesh):
    placed = (
        P("clip", "shard", None),
        P("clip", None, "shard"),
        P(),
        P(("clip", "shard"), None, None),
        P(("clip", "shard"), None),
        P(("clip", "shard"), None, None),
        P(("clip", "shard"), None),
    )
    return jax.shard_map(
        local, mesh=mesh, in_specs=placed, out_specs=P("clip", "shard", None), check_vma=False
    )
```

profile of v0, /device:TPU:0, one launch (start us, length us, event | category | flops | bytes accessed | tf_op | source)
XLA Modules:
  0.0 90.1 jit_solution(5664969865137726673)
XLA Ops:
  0.0 0.0 copy-start
  0.0 0.9 copy.50
  0.9 5.7 %copy.30 = bf16[1,2304,768]{1,2,0:T(8,128)(2,1)} copy(bf16[1,2304,768]{2,1,0:T(8,128)(2,1)} %param.7) | data formatting | bytes 7077888 | tf_op args[0]
  6.6 2.8 %fusion.4 = bf16[2304,768]{0,1:T(8,128)(2,1)S(1)} fusion(f32[2304,6]{0,1:T(8,128)S(1)} %bitcast.124, bf16[1,2304,768]{1,2,0:T(8,128)(2,1)} %copy.30), kind=kLoop, calls=%fused_computation.5 | loop fusion | flops 5308416 | bytes 7133184 | tf_op jit(solution)/shard_map/convert_element_type | solution.py:36
  9.4 0.3 copy-done.1
  9.7 2.4 %multiply_convert_fusion = bf16[2304,6,128]{0,2,1:T(8,128)(2,1)} fusion(f32[2304,6]{0,1:T(8,128)S(1)} %bitcast.125, bf16[2304,6,128]{0,2,1:T(8,128)(2,1)S(1)} %bitcast.118), kind=kLoop, calls=%fused_computation.6 | loop fusion | flops 5308416 | bytes 7133184 | tf_op jit(solution)/shard_map/convert_element_type | solution.py:36
  12.1 0.0 copy-done
  12.1 0.8 fusion.46
  12.9 13.5 %pmax.7 = f32[128]{0:T(128)S(1)} all-reduce(f32[128]{0:T(128)S(1)} %get-tuple-element.8), channel_id=1, replica_groups=mesh['clip'=8,'shard'=4] {'shard'}, use_global_device_ids=true, to_apply=%region_3.0 | all-reduce | flops 128 | bytes 1024 | tf_op jit(solution)/shard_map/pmax | solution.py:43
  26.4 0.4 fusion.18
  26.8 8.4 %psum.7 = f32[128]{0:T(128)S(1)} all-reduce(f32[128]{0:T(128)S(1)} %get-tuple-element.6), channel_id=1, replica_groups=mesh['clip'=8,'shard'=4] {'shard'}, use_global_device_ids=true, to_apply=%region_5.0 | all-reduce | flops 128 | bytes 1024 | tf_op jit(solution)/shard_map/psum | solution.py:44
  35.1 0.3 fusion.24
  35.5 0.0 copy-start.2
  35.5 0.0 copy-start.3
  35.5 0.1 dot_general.18
  35.6 3.3 %fusion.20 = f32[32,4,768]{2,0,1:T(8,128)S(1)} fusion(bf16[2304,768,1]{0,1,2:T(8,128)(2,1)} %bitcast.121, bf16[32,4,2304]{2,1,0:T(4,128)(2,1)S(1)} %dot_general.18), kind=kOutput, calls=%fused_computation.20 | convolution fusion | flops 452984832 | bytes 4521984 | tf_op jit(solution)/shard_map/dot_general | solution.py:46
  38.9 1.0 %copy.33 = f32[32,4,768]{2,1,0:T(4,128)} copy(f32[32,4,768]{2,0,1:T(8,128)S(1)} %fusion.20) | data formatting | bytes 786432 | tf_op jit(solution)/shard_map/dot_general | solution.py:46
  39.9 4.2 %all-to-all-start = ((f32[32,4,768]{2,1,0:T(4,128)}), f32[32,4,768]{2,1,0:T(4,128)S(1)}, u32[]{:S(2)}, u32[]{:S(2)}) async-start(f32[32,4,768]{2,1,0:T(4,128)} %copy.33), calls=%async_computation | async-start | bytes 786432 | tf_op jit(solution)/shard_map/all_to_all | solution.py:49
  44.2 0.0 copy-done.2
  44.2 11.8 %all-to-all-done = f32[32,4,768]{2,1,0:T(4,128)S(1)} async-done(((f32[32,4,768]{2,1,0:T(4,128)}), f32[32,4,768]{2,1,0:T(4,128)S(1)}, u32[]{:S(2)}, u32[]{:S(2)}) %all-to-all-start) | async-done | bytes 393248 | tf_op jit(solution)/shard_map/all_to_all | solution.py:49
  56.0 0.1 bitcast_reduce_fusion
  56.1 0.1 multiply_reduce_fusion
  56.2 0.1 copy.34
  56.3 5.8 %fusion.27 = bf16[8,2,2,3072]{3,0,2,1:T(8,128)(2,1)S(1)} fusion(bf16[2,768,3072]{2,1,0:T(8,128)(2,1)} %param.10, f32[2,3072]{1,0:T(2,128)S(1)} %convert_element_type.94, f32[8,2,2,768]{3,0,2,1:T(8,128)S(1)} %bitcast.126, f32[8,2,2]{0,2,1:T(2,128)S(1)} %bitcast.127), kind=kOutput, calls=%fused_computation.27 | convolution fusion | flops 157532160 | bytes 9756800 | tf_op jit(solution)/shard_map/cisd,idf->cisf/dot_general | solution.py:12
  62.1 0.4 slice-done.2
  62.5 1.3 %fusion.15 = bf16[8,2,2,768]{3,0,2,1:T(8,128)(2,1)S(1)} fusion(bf16[8,2,2,3072]{3,0,2,1:T(8,128)(2,1)S(1)} %fusion.27, bf16[2,3072,768]{2,1,0:T(8,128)(2,1)S(1)} %bitcast.120, f32[2,768]{1,0:T(2,128)S(1)} %convert_element_type.96), kind=kOutput, calls=%fused_computation.16 | convolution fusion | flops 151044096 | bytes 9689088 | tf_op jit(solution)/shard_map/cisf,ifd->cisd/dot_general | solution.py:18
  63.9 13.9 %all_gather.3 = bf16[4,32,768]{2,1,0:T(8,128)(2,1)S(1)} all-gather(bf16[1,32,768]{2,1,0:T(8,128)(2,1)S(1)} %reshape.65), channel_id=1, replica_groups=mesh['clip'=8,'shard'=4] {'shard'}, dimensions={0}, use_global_device_ids=true | all-gather | bytes 245760 | tf_op jit(solution)/shard_map/all_gather | solution.py:62
  77.8 0.2 copy.37
  78.0 9.0 %all_to_all.21 = bf16[4,32,768]{2,0,1:T(4,128)(2,1)S(1)} all-to-all(bf16[4,32,768]{2,0,1:T(4,128)(2,1)S(1)} %copy.37), channel_id=1, replica_groups=mesh['clip'=8,'shard'=4] {'clip'}, dimensions={1} | all-to-all | bytes 393216 | tf_op jit(solution)/shard_map/all_to_all | solution.py:65
  87.0 0.1 copy.49
  87.1 0.1 reshape.66
  87.1 2.9 %fusion.5 = bf16[1,2304,768]{2,1,0:T(8,128)(2,1)} fusion(bf16[128,768]{1,0:T(8,128)(2,1)S(1)} %reshape.66, f32[2304,128]{0,1:T(8,128)S(1)} %get-tuple-element.9, f32[2304]{0:T(1024)S(1)} %get-tuple-element.5, f32[2304]{0:T(1024)S(1)} %get-tuple-element.7), kind=kOutput, calls=%fused_computation.8 | convolution fusion | flops 455639040 | bytes 4933632 | tf_op jit(solution)/shard_map/dot_general | solution.py:66
  (14 shorter events, 0.1 us)
Async XLA Ops:
  0.0 12.1 %copy-start = (bf16[768,128]{1,0:T(8,128)(2,1)S(1)}, bf16[768,128]{1,0:T(8,128)(2,1)}, u32[]{:S(2)}) copy-start(bf16[768,128]{1,0:T(8,128)(2,1)} %param.9) | copy-start | bytes 589828
  6.6 3.1 %copy-start.1 = (bf16[1,2304,768]{1,2,0:T(8,128)(2,1)S(1)}, bf16[1,2304,768]{1,2,0:T(8,128)(2,1)}, u32[]{:S(2)}) copy-start(bf16[1,2304,768]{1,2,0:T(8,128)(2,1)} %copy.30) | copy-start | bytes 10616836
  35.5 8.7 %copy-start.2 = (bf16[2,3072]{1,0:T(2,128)(2,1)S(1)}, bf16[2,3072]{1,0:T(2,128)(2,1)}, u32[]{:S(2)}) copy-start(bf16[2,3072]{1,0:T(2,128)(2,1)} %param.11) | copy-start | bytes 36868
  35.5 8.7 %copy-start.3 = (bf16[2,768]{1,0:T(2,128)(2,1)S(1)}, bf16[2,768]{1,0:T(2,128)(2,1)}, u32[]{:S(2)}) copy-start(bf16[2,768]{1,0:T(2,128)(2,1)} %param.13) | copy-start | bytes 9220
  39.9 16.1 %all-to-all-start = ((f32[32,4,768]{2,1,0:T(4,128)}), f32[32,4,768]{2,1,0:T(4,128)S(1)}, u32[]{:S(2)}, u32[]{:S(2)}) async-start(f32[32,4,768]{2,1,0:T(4,128)} %copy.33), calls=%async_computation | async-start | bytes 786432 | tf_op jit(solution)/shard_map/all_to_all | solution.py:49
  56.0 6.0 %slice-start = ((s8[9437184]{0:T(1024)(128)(4,1)}), s8[1048576]{0:T(1024)(128)(4,1)S(1)}, s32[]{:S(2)}) async-start(s8[9437184]{0:T(1024)(128)(4,1)} %bitcast.119), calls=%async_computation.2 | async-start | bytes 2097152
  56.3 5.8 %slice-start.1 = ((s8[9437184]{0:T(1024)(128)(4,1)}), s8[4194304]{0:T(1024)(128)(4,1)S(1)}, s32[]{:S(2)}) async-start(s8[9437184]{0:T(1024)(128)(4,1)} %bitcast.119), calls=%async_computation.3 | async-start | bytes 8388608
  56.3 6.2 %slice-start.2 = ((s8[9437184]{0:T(1024)(128)(4,1)}), s8[4194304]{0:T(1024)(128)(4,1)S(1)}, s32[]{:S(2)}) async-start(s8[9437184]{0:T(1024)(128)(4,1)} %bitcast.119), calls=%async_computation.4 | async-start | bytes 8388608
where the time goes:
time: 90.5 us; the launch traced here: 90.1 us
  blocking collectives  44.7 us (49%)
  matrix products  14.1 us (16%)
  waiting for transfers between devices  11.8 us (13%)
  local copies, waits for them, and re-layouts  8.94 us (10%)
  other arithmetic  6.13 us (7%)
  starting transfers between devices  4.25 us (5%)
    all_gather x1, blocking collectives, local(): lax.all_gather(slot_outputs.reshape(1, clip_count * owner_rows, feature_d...  13.9 us
    pmax x1, blocking collectives, local(): column_peak = lax.pmax(jnp.max(logits, axis=0), 'shard')  13.5 us
    all_to_all x1, waiting for transfers between devices, local(): lax.all_to_all(partial_value, ('clip', 'shard'), split_axis=0, concat_axi...  11.8 us
    all_to_all x1, blocking collectives, local(): lax.all_to_all(gathered, 'clip', split_axis=1, concat_axis=0, tiled=True)  9.01 us
    psum x1, blocking collectives, local(): lax.psum(jnp.sum(jnp.exp(logits - column_peak), axis=0), 'shard')  8.37 us
    unnamed x16, local copies, waits for them, and re-layouts  7.36 us
    dot_general x1, matrix products, expert_apply(): jnp.einsum('cisd,idf->cisf', normalized, expand_weight, preferred_element...  5.76 us
    convert_element_type x2, other arithmetic, local(): features = features.reshape(token_count, feature_dim).astype(jnp.bfloat16)  5.22 us
  transfers between devices with their start and end apart: 1, of which 1 were waited for; matrix products, arithmetic and copies ran while one was open for 0% of the time, Pallas kernels for 0%

commit v1 on v0

v1 whole, which is shorter than its diff:
```python
import functools
import math

import jax
import jax.numpy as jnp
from jax import lax
from jax.experimental import pallas as pl
from jax.experimental.pallas import tpu as pltpu
from jax.sharding import PartitionSpec as P

F32 = jnp.float32
BF16 = jnp.bfloat16
MESH = pl.DeviceIdType.MESH
CHUNK = 256
HIDDEN_CHUNK = 768


def dot(a, b, contract=((1,), (0,))):
    return lax.dot_general(a, b, (contract, ((), ())), preferred_element_type=F32)


def iota(shape, axis):
    return lax.broadcasted_iota(jnp.int32, shape, axis)


def spread_matrix(groups, rows, piece, parts):
    shape = (groups * rows * parts, groups * rows)
    out, row = iota(shape, 0), iota(shape, 1)
    wide = rows * parts
    target = (row // rows) * wide + piece * rows + row % rows
    return (out == target).astype(F32).astype(BF16)


def gather_matrix(groups, rows, piece, parts):
    shape = (groups * rows, groups * rows * parts)
    row, out = iota(shape, 0), iota(shape, 1)
    wide = rows * parts
    target = (row // rows) * wide + piece * rows + row % rows
    return (out == target).astype(F32).astype(BF16)


def kernel(
    clips,
    shards,
    tokens,
    scales,
    slot_params,
    w1,
    b1,
    w2,
    b2,
    combine,
    returned,
    feat,
    scale_v,
    params_v,
    w1_v,
    b1_v,
    w2_v,
    b2_v,
    logits,
    stats,
    partial,
    sums,
    out_rows,
    in_rows,
    back_out,
    back_in,
    gathered,
    local_sem,
    token_sem,
    send_a,
    recv_a,
    send_b,
    recv_b,
    send_c,
    recv_c,
    send_d,
    recv_d,
    send_e,
    recv_e,
):
    c_me, s_me = lax.axis_index("clip"), lax.axis_index("shard")
    count, dim = feat.shape
    blocks = scale_v.shape[0]
    width = dim // blocks
    slots = params_v.shape[1]
    experts, _, ff = w1_v.shape
    rows = slots // (clips * shards)
    each = rows // experts
    group = clips * rows
    parts = in_rows.shape[1] // rows
    piece_dim = dim // parts
    chunks = count // CHUNK

    def span(i):
        return pl.ds(pl.multiple_of(i * CHUNK, CHUNK), CHUNK)

    load_scale = pltpu.make_async_copy(scales, scale_v, local_sem.at[0])
    load_params = pltpu.make_async_copy(slot_params, params_v, local_sem.at[1])
    load_params.start()
    load_scale.start()
    for i in range(chunks):
        pltpu.make_async_copy(
            tokens.at[pl.ds(i * CHUNK, CHUNK)], feat.at[pl.ds(i * CHUNK, CHUNK)], token_sem.at[i]
        ).start()
    weight_loads = [
        pltpu.make_async_copy(w1, w1_v, local_sem.at[2]),
        pltpu.make_async_copy(b1, b1_v, local_sem.at[3]),
        pltpu.make_async_copy(w2, w2_v, local_sem.at[4]),
        pltpu.make_async_copy(b2, b2_v, local_sem.at[5]),
    ]
    for load in weight_loads:
        load.start()

    barrier = pltpu.get_barrier_semaphore()
    for d in range(1, shards):
        pl.semaphore_signal(
            barrier, inc=1, device_id=(c_me, lax.rem(s_me + d, shards)), device_id_type=MESH
        )
    for d in range(1, clips):
        pl.semaphore_signal(
            barrier, inc=1, device_id=(lax.rem(c_me + d, clips), s_me), device_id_type=MESH
        )

    load_params.wait()
    shape = (slots, slots)
    old, new = iota(shape, 0), iota(shape, 1)
    source = (((new % group) // rows) * shards + new // group) * rows + new % rows
    ordered = dot(params_v[...], (old == source).astype(F32).astype(BF16)).astype(BF16)
    params_v[...] = ordered
    load_scale.wait()

    def logits_step(i, peak):
        at = span(i)
        pltpu.make_async_copy(tokens.at[at], feat.at[at], token_sem.at[i]).wait()
        scale = scale_v[:, at].T
        for b in range(blocks):
            lanes = slice(b * width, (b + 1) * width)
            feat[at, lanes] = (feat[at, lanes].astype(F32) * scale[:, b : b + 1]).astype(BF16)
        value = dot(feat[at, :], params_v[...])
        logits[at, :] = value
        return jnp.maximum(peak, jnp.max(value, axis=0, keepdims=True))

    peak = lax.fori_loop(0, chunks, logits_step, jnp.full((1, slots), -jnp.inf, F32))

    def sum_step(i, total):
        return total + jnp.sum(jnp.exp(logits[span(i), :] - peak), axis=0, keepdims=True)

    total = lax.fori_loop(0, chunks, sum_step, jnp.zeros((1, slots), F32))
    which = iota((8, slots), 0)
    stats[s_me] = jnp.where(which == 0, peak, total)

    pl.semaphore_wait(barrier, shards - 1 + clips - 1)

    def shard_copies(make):
        return [make(d, lax.rem(s_me + d, shards)) for d in range(1, shards)]

    def clip_copies(make):
        return [make(d, lax.rem(c_me + d, clips)) for d in range(1, clips)]

    stats_sent = shard_copies(
        lambda d, to: pltpu.make_async_remote_copy(
            src_ref=stats.at[s_me],
            dst_ref=stats.at[s_me],
            send_sem=send_a.at[d],
            recv_sem=recv_a.at[s_me],
            device_id=(c_me, to),
            device_id_type=MESH,
        )
    )
    for copy in stats_sent:
        copy.start()

    def combine_step(i, carry):
        at = span(i)
        value = logits[at, :]
        weights = jnp.exp(value - jnp.max(value, axis=1, keepdims=True))
        combine[at, :] = (weights / jnp.sum(weights, axis=1, keepdims=True)).astype(BF16)
        return carry

    lax.fori_loop(0, chunks, combine_step, 0)

    def arrivals(me, size, ref, recv):
        for d in range(1, size):
            origin = lax.rem(me + d, size)
            pltpu.make_async_copy(ref.at[origin], ref.at[origin], recv.at[origin]).wait()

    arrivals(s_me, shards, stats, recv_a)
    top = stats[0, 0:1, :]
    for s in range(1, shards):
        top = jnp.maximum(top, stats[s, 0:1, :])
    total = jnp.zeros((1, slots), F32)
    for s in range(shards):
        total = total + stats[s, 1:2, :] * jnp.exp(stats[s, 0:1, :] - top)

    partial[...] = jnp.zeros(partial.shape, F32)

    def partial_step(i, carry):
        at = span(i)
        dispatch = (jnp.exp(logits[at, :] - top) / total).astype(BF16)
        part = dot(dispatch, feat[at, :], ((0,), (0,)))
        partial[...] += part.reshape(partial.shape)
        return carry

    lax.fori_loop(0, chunks, partial_step, 0)

    sums_sent = shard_copies(
        lambda d, to: pltpu.make_async_remote_copy(
            src_ref=partial.at[to],
            dst_ref=sums.at[s_me],
            send_sem=send_b.at[d],
            recv_sem=recv_b.at[s_me],
            device_id=(c_me, to),
            device_id_type=MESH,
        )
    )
    for copy in sums_sent:
        copy.start()
    sums[s_me] = partial[s_me]
    arrivals(s_me, shards, sums, recv_b)
    value = sums[0]
    for s in range(1, shards):
        value = value + sums[s]
    value = value.astype(BF16)

    def spread(value):
        spreads = [
            dot(
                spread_matrix(clips, rows, p, parts),
                value[:, p * piece_dim : (p + 1) * piece_dim],
            )
            for p in range(parts)
        ]
        return sum(spreads[1:], spreads[0]).reshape(clips, rows * parts, piece_dim)

    def unspread(value):
        value = value.reshape(clips * rows * parts, piece_dim).astype(BF16)
        return jnp.concatenate(
            [dot(gather_matrix(clips, rows, p, parts), value) for p in range(parts)], axis=1
        )

    def exchange(source, target, send, recv):
        target[c_me] = source[c_me]
        sent = clip_copies(
            lambda d, to: pltpu.make_async_remote_copy(
                src_ref=source.at[to],
                dst_ref=target.at[c_me],
                send_sem=send.at[d],
                recv_sem=recv.at[c_me],
                device_id=(to, s_me),
                device_id_type=MESH,
            )
        )
        for copy in sent:
            copy.start()
        arrivals(c_me, clips, target, recv)
        return sent

    out_rows[...] = spread(value)
    rows_sent = exchange(out_rows, in_rows, send_c, recv_c)

    wide = unspread(in_rows[...])
    mean = jnp.mean(wide * wide, axis=-1, keepdims=True)
    normalized = (wide * lax.rsqrt(mean + 1e-06)).astype(BF16)
    for load in weight_loads:
        load.wait()

    def mine(shape, expert):
        return (iota(shape, 0) % rows) // each == expert

    def choose(values):
        chosen = values[0]
        for e in range(1, experts):
            chosen = jnp.where(mine(chosen.shape, e), values[e], chosen)
        return chosen

    def spread_bias(ref, at):
        value = ref[:, at].astype(F32)
        size = (group, value.shape[1])
        return choose([jnp.broadcast_to(value[e : e + 1], size) for e in range(experts)])

    def expert_step(f, outs):
        at = pl.ds(pl.multiple_of(f * HIDDEN_CHUNK, HIDDEN_CHUNK), HIDDEN_CHUNK)
        before = choose([dot(normalized, w1_v[e, :, at]) for e in range(experts)])
        before = before + spread_bias(b1_v, at)
        hidden = (0.5 * before * (1.0 + lax.erf(before * math.sqrt(0.5)))).astype(BF16)
        return tuple(outs[e] + dot(hidden, w2_v[e, at, :]) for e in range(experts))

    outs = tuple(jnp.zeros((group, dim), F32) for _ in range(experts))
    outs = lax.fori_loop(0, ff // HIDDEN_CHUNK, expert_step, outs)
    result = (choose(outs) + spread_bias(b2_v, slice(None))).astype(BF16)

    back_out[...] = spread(result)
    back_sent = exchange(back_out, back_in, send_d, recv_d)
    gathered[s_me] = unspread(back_in[...]).astype(BF16)
    last_sent = shard_copies(
        lambda d, to: pltpu.make_async_remote_copy(
            src_ref=gathered.at[s_me],
            dst_ref=gathered.at[s_me],
            send_sem=send_e.at[d],
            recv_sem=recv_e.at[s_me],
            device_id=(c_me, to),
            device_id_type=MESH,
        )
    )
    for copy in last_sent:
        copy.start()
    arrivals(s_me, shards, gathered, recv_e)
    returned[...] = gathered[...].reshape(returned.shape)
    for copy in stats_sent + sums_sent + rows_sent + back_sent + last_sent:
        copy.wait_send()


def local(clips, shards, tokens, scales, slot_params, w1, b1, w2, b2):
    count, dim = tokens.shape[1:]
    blocks = scales.shape[1]
    slots = slot_params.shape[1]
    rows = slots // (clips * shards)
    group = clips * rows
    parts = 8 // rows
    piece = (clips, rows * parts, dim // parts)
    combine, returned = pl.pallas_call(
        functools.partial(kernel, clips, shards),
        out_shape=(
            jax.ShapeDtypeStruct((count, slots), BF16),
            jax.ShapeDtypeStruct((slots, dim), BF16),
        ),
        in_specs=[pl.BlockSpec(memory_space=pl.ANY)] * 7,
        out_specs=(pl.BlockSpec(memory_space=pltpu.VMEM),) * 2,
        scratch_shapes=[
            pltpu.VMEM((count, dim), BF16),
            pltpu.VMEM((blocks, count), F32),
            pltpu.VMEM(slot_params.shape, BF16),
            pltpu.VMEM(w1.shape, BF16),
            pltpu.VMEM(b1.shape, BF16),
            pltpu.VMEM(w2.shape, BF16),
            pltpu.VMEM(b2.shape, BF16),
            pltpu.VMEM((count, slots), F32),
            pltpu.VMEM((shards, 8, slots), F32),
            pltpu.VMEM((shards, group, dim), F32),
            pltpu.VMEM((shards, group, dim), F32),
            pltpu.VMEM(piece, F32),
            pltpu.VMEM(piece, F32),
            pltpu.VMEM(piece, F32),
            pltpu.VMEM(piece, F32),
            pltpu.VMEM((shards, group, dim), BF16),
            pltpu.SemaphoreType.DMA((6,)),
            pltpu.SemaphoreType.DMA((count // CHUNK,)),
            pltpu.SemaphoreType.DMA((shards,)),
            pltpu.SemaphoreType.DMA((shards,)),
            pltpu.SemaphoreType.DMA((shards,)),
            pltpu.SemaphoreType.DMA((shards,)),
            pltpu.SemaphoreType.DMA((clips,)),
            pltpu.SemaphoreType.DMA((clips,)),
            pltpu.SemaphoreType.DMA((clips,)),
            pltpu.SemaphoreType.DMA((clips,)),
            pltpu.SemaphoreType.DMA((shards,)),
            pltpu.SemaphoreType.DMA((shards,)),
        ],
        compiler_params=pltpu.CompilerParams(
            collective_id=0, has_side_effects=True, vmem_limit_bytes=56 << 20
        ),
        name="slots",
    )(tokens[0], scales[0], slot_params, w1, b1, w2, b2)
    mixed = jnp.dot(combine, returned, preferred_element_type=F32).astype(BF16)
    return mixed[None]


def solution(mesh):
    placed = (
        P("clip", "shard", None),
        P("clip", None, "shard"),
        P(),
        P(("clip", "shard"), None, None),
        P(("clip", "shard"), None),
        P(("clip", "shard"), None, None),
        P(("clip", "shard"), None),
    )
    return jax.shard_map(
        functools.partial(local, mesh.shape["clip"], mesh.shape["shard"]),
        mesh=mesh,
        in_specs=placed,
        out_specs=P("clip", "shard", None),
        check_vma=False,
    )
```

time: 90.5 us -> 50.1 us (0.55)
  blocking collectives: 44.7 us -> 0 us
  Pallas kernels: 0 us -> 44.5 us
  waiting for transfers between devices: 11.8 us -> 0 us
  matrix products: 14.1 us -> 3.97 us
  local copies, waits for them, and re-layouts: 8.94 us -> 1.45 us
  other arithmetic: 6.13 us -> 0 us
  starting transfers between devices: 4.25 us -> 0 us
    pallas_call x0 -> x1, Pallas kernels: none -> 44.5 us  [local(): pl.pallas_call(functools.partial(kernel, clips, shards), out_shape=(jax.S...]
    all_gather x1 -> x0, blocking collectives: 13.9 us -> none  [local(): lax.all_gather(slot_outputs.reshape(1, clip_count * owner_rows, feature_d...]
    pmax x1 -> x0, blocking collectives: 13.5 us -> none  [local(): column_peak = lax.pmax(jnp.max(logits, axis=0), 'shard')]
    all_to_all x1 -> x0, waiting for transfers between devices: 11.8 us -> none  [local(): lax.all_to_all(partial_value, ('clip', 'shard'), split_axis=0, concat_axi...]
    dot_general x5 -> x1, matrix products: 14.1 us -> 3.97 us  [local(): mixed = jnp.dot(combine, returned, preferred_element_type=F32).astype(BF16)]
    all_to_all x1 -> x0, blocking collectives: 9.01 us -> none  [local(): lax.all_to_all(gathered, 'clip', split_axis=1, concat_axis=0, tiled=True)]
    psum x1 -> x0, blocking collectives: 8.37 us -> none  [local(): lax.psum(jnp.sum(jnp.exp(logits - column_peak), axis=0), 'shard')]
    unnamed x16 -> x1, local copies, waits for them, and re-layouts: 7.36 us -> 1.45 us
  transfers between devices with their start and end apart: 1 -> 0, of which waited for: 1 -> 0; matrix products, arithmetic and copies ran while one was open for 0% -> 0% of each run, Pallas kernels for 0% -> 0%
where the time goes in v1:
time: 50.1 us; the launch traced here: 49.9 us
  Pallas kernels  44.5 us (89%)
  matrix products  3.97 us (8%)
  local copies, waits for them, and re-layouts  1.45 us (3%)
    pallas_call x1, Pallas kernels, local(): pl.pallas_call(functools.partial(kernel, clips, shards), out_shape=(jax.S...  44.5 us
    dot_general x1, matrix products, local(): mixed = jnp.dot(combine, returned, preferred_element_type=F32).astype(BF16)  3.97 us
    unnamed x1, local copies, waits for them, and re-layouts  1.45 us

profile of v1, /device:TPU:0, one launch (start us, length us, event | category | flops | bytes accessed | tf_op | source)
XLA Modules:
  0.0 49.9 jit_solution(3958904692716800790)
XLA Ops:
  0.0 1.5 %copy.10 = f32[1,6,2304]{2,1,0:T(8,128)} copy(f32[1,6,2304]{2,0,1:T(1,128)} %param.8) | data formatting | bytes 110592
  1.5 44.5 %slots.1 = (bf16[2304,128]{1,0:T(8,128)(2,1)}, bf16[128,768]{1,0:T(8,128)(2,1)}) custom-call(bf16[2304,768]{1,0:T(8,128)(2,1)} %bitcast.8, f32[6,2304]{1,0:T(8,128)} %bitcast.9, bf16[768,128]{1,0:T(8,128)(2,1)} %slot_params.1, bf16[2,768,3072]{2,1,0:T(8,128)(2,1)} %w1.1, bf16[2,3072]{1,0:T(2,128)(2,1)} %b1.1, bf16[2,3072,768]{2,1,0:T(8,128)(2,1)} %w2.1, ...), custom_call_target="tpu_custom_call" | custom-call | tf_op jit(solution)/shard_map/slots/pallas_call | solution.py:323
  46.0 4.0 %fusion = bf16[1,2304,768]{2,1,0:T(8,128)(2,1)} fusion(bf16[2304,128]{1,0:T(8,128)(2,1)} %get-tuple-element.7, bf16[128,768]{1,0:T(8,128)(2,1)} %get-tuple-element.8), kind=kOutput, calls=%fused_computation.1 | convolution fusion | flops 454754304 | bytes 4325376 | tf_op jit(solution)/shard_map/dot_general | solution.py:366

commit v2 on v1

v2 whole, which is shorter than its diff:
```python
import functools
import math

import jax
import jax.numpy as jnp
from jax import lax
from jax.experimental import pallas as pl
from jax.experimental.pallas import tpu as pltpu
from jax.sharding import PartitionSpec as P

F32 = jnp.float32
BF16 = jnp.bfloat16
MESH = pl.DeviceIdType.MESH
CHUNK = 256
HIDDEN_CHUNK = 768
MIX_ROWS = 384


def dot(a, b, contract=((1,), (0,))):
    return lax.dot_general(a, b, (contract, ((), ())), preferred_element_type=F32)


def iota(shape, axis):
    return lax.broadcasted_iota(jnp.int32, shape, axis)


def top_half(shape, rows):
    return iota(shape, 0) % (2 * rows) < rows


def spread(value, rows):
    count, dim = value.shape
    left, right = value[:, : dim // 2], value[:, dim // 2 :]
    top = top_half(left.shape, rows)
    even = jnp.where(top, left, pltpu.roll(right, rows, 0))
    odd = jnp.where(top, pltpu.roll(left, count - rows, 0), right)
    shape = (count // (2 * rows), 2 * rows, dim // 2)
    return even.reshape(shape), odd.reshape(shape)


def unspread(even, odd, rows):
    shape = (even.shape[0] * 2 * rows, even.shape[2])
    even, odd = even.reshape(shape), odd.reshape(shape)
    top = top_half(shape, rows)
    left = jnp.where(top, even, pltpu.roll(odd, rows, 0))
    right = jnp.where(top, pltpu.roll(even, shape[0] - rows, 0), odd)
    return jnp.concatenate([left, right], axis=1)


def kernel(
    clips,
    shards,
    tokens,
    scales,
    slot_params,
    w1,
    b1,
    w2,
    b2,
    combine,
    returned,
    feat,
    scale_v,
    params_v,
    w1_v,
    b1_v,
    w2_v,
    b2_v,
    logits,
    lifted,
    combine_v,
    stats,
    partial,
    partial_out,
    sums,
    back_out,
    back_in,
    local_sem,
    token_sem,
    send_a,
    recv_a,
    send_b,
    recv_b,
    send_c,
    recv_c,
):
    c_me, s_me = lax.axis_index("clip"), lax.axis_index("shard")
    count, dim = feat.shape
    blocks = scale_v.shape[0]
    width = dim // blocks
    slots = params_v.shape[1]
    experts, _, ff = w1_v.shape
    rows = slots // (clips * shards)
    each = rows // experts
    group = clips * rows
    devices = clips * shards
    me = c_me * shards + s_me
    chunks = count // CHUNK

    def span(i):
        return pl.ds(pl.multiple_of(i * CHUNK, CHUNK), CHUNK)

    load_scale = pltpu.make_async_copy(scales, scale_v, local_sem.at[0])
    load_params = pltpu.make_async_copy(slot_params, params_v, local_sem.at[1])
    load_params.start()
    load_scale.start()
    for i in range(chunks):
        pltpu.make_async_copy(
            tokens.at[pl.ds(i * CHUNK, CHUNK)], feat.at[pl.ds(i * CHUNK, CHUNK)], token_sem.at[i]
        ).start()
    weight_loads = [
        pltpu.make_async_copy(w1, w1_v, local_sem.at[2]),
        pltpu.make_async_copy(b1, b1_v, local_sem.at[3]),
        pltpu.make_async_copy(w2, w2_v, local_sem.at[4]),
        pltpu.make_async_copy(b2, b2_v, local_sem.at[5]),
    ]
    for load in weight_loads:
        load.start()

    barrier = pltpu.get_barrier_semaphore()

    def place(d):
        at = lax.rem(me + d, devices)
        return at, at // shards, lax.rem(at, shards)

    def greet(d, carry):
        _, c, s = place(d)
        pl.semaphore_signal(barrier, inc=1, device_id=(c, s), device_id_type=MESH)
        return carry

    lax.fori_loop(1, devices, greet, 0)
    load_params.wait()
    load_scale.wait()

    def logits_step(i, peak):
        at = span(i)
        pltpu.make_async_copy(tokens.at[at], feat.at[at], token_sem.at[i]).wait()
        scale = scale_v[:, 0, at].T
        for b in range(blocks):
            lanes = slice(b * width, (b + 1) * width)
            feat[at, lanes] = (feat[at, lanes].astype(F32) * scale[:, b : b + 1]).astype(BF16)
        value = dot(feat[at, :], params_v[...])
        logits[at, :] = value
        return jnp.maximum(peak, jnp.max(value, axis=0, keepdims=True))

    peak = lax.fori_loop(0, chunks, logits_step, jnp.full((1, slots), -jnp.inf, F32))

    def sum_step(i, total):
        at = span(i)
        value = jnp.exp(logits[at, :] - peak)
        lifted[at, :] = value
        return total + jnp.sum(value, axis=0, keepdims=True)

    total = lax.fori_loop(0, chunks, sum_step, jnp.zeros((1, slots), F32))
    which = iota((8, slots), 0)
    stats[s_me] = jnp.where(which == 0, peak, total)

    pl.semaphore_wait(barrier, devices - 1)

    def shard_copies(make):
        return [make(d, lax.rem(s_me + d, shards)) for d in range(1, shards)]

    stats_sent = shard_copies(
        lambda d, to: pltpu.make_async_remote_copy(
            src_ref=stats.at[s_me],
            dst_ref=stats.at[s_me],
            send_sem=send_a.at[d],
            recv_sem=recv_a.at[s_me],
            device_id=(c_me, to),
            device_id_type=MESH,
        )
    )
    for copy in stats_sent:
        copy.start()

    for d in range(1, shards):
        origin = lax.rem(s_me + d, shards)
        pltpu.make_async_copy(stats.at[origin], stats.at[origin], recv_a.at[origin]).wait()
    top = stats[0, 0:1, :]
    for s in range(1, shards):
        top = jnp.maximum(top, stats[s, 0:1, :])
    total = jnp.zeros((1, slots), F32)
    for s in range(shards):
        total = total + stats[s, 1:2, :] * jnp.exp(stats[s, 0:1, :] - top)

    lift = jnp.exp(peak - top) / total
    partial[...] = jnp.zeros(partial.shape, F32)

    def partial_step(i, carry):
        at = span(i)
        dispatch = (lifted[at, :] * lift).astype(BF16)
        partial[...] += dot(dispatch, feat[at, :], ((0,), (0,)))
        return carry

    lax.fori_loop(0, chunks, partial_step, 0)
    even, odd = spread(partial[...], rows)
    partial_out[:, 0] = even
    partial_out[:, 1] = odd

    def send_sum(d):
        to, c, s = place(d)
        return pltpu.make_async_remote_copy(
            src_ref=partial_out.at[to // 2, lax.rem(to, 2)],
            dst_ref=sums.at[s_me, c_me // 2, lax.rem(c_me, 2)],
            send_sem=send_b.at[d],
            recv_sem=recv_b.at[me],
            device_id=(c, s),
            device_id_type=MESH,
        )

    def start_sum(d, carry):
        send_sum(d).start()
        return carry

    lax.fori_loop(1, devices, start_sum, 0)
    sums[s_me, c_me // 2, lax.rem(c_me, 2)] = partial_out[me // 2, lax.rem(me, 2)]

    def combine_step(i, carry):
        at = span(i)
        value = logits[at, :]
        weights = jnp.exp(value - jnp.max(value, axis=1, keepdims=True))
        combine_v[at, :] = (weights / jnp.sum(weights, axis=1, keepdims=True)).astype(BF16)
        return carry

    lax.fori_loop(0, chunks, combine_step, 0)
    store = pltpu.make_async_copy(combine_v, combine, local_sem.at[6])
    store.start()

    def await_sum(d, carry):
        origin, c, s = place(d)
        landed = sums.at[s, c // 2, lax.rem(c, 2)]
        pltpu.make_async_copy(landed, landed, recv_b.at[origin]).wait()
        return carry

    lax.fori_loop(1, devices, await_sum, 0)
    value = sums[0]
    for s in range(1, shards):
        value = value + sums[s]
    wide = unspread(value[:, 0], value[:, 1], rows).astype(BF16).astype(F32)

    mean = jnp.mean(wide * wide, axis=-1, keepdims=True)
    normalized = (wide * lax.rsqrt(mean + 1e-06)).astype(BF16)
    for load in weight_loads:
        load.wait()

    def mine(shape, expert):
        return (iota(shape, 0) % rows) // each == expert

    def choose(values):
        chosen = values[0]
        for e in range(1, experts):
            chosen = jnp.where(mine(chosen.shape, e), values[e], chosen)
        return chosen

    def spread_bias(ref, at):
        value = ref[:, at].astype(F32)
        size = (group, value.shape[1])
        return choose([jnp.broadcast_to(value[e : e + 1], size) for e in range(experts)])

    def expert_step(f, outs):
        at = pl.ds(pl.multiple_of(f * HIDDEN_CHUNK, HIDDEN_CHUNK), HIDDEN_CHUNK)
        before = choose([dot(normalized, w1_v[e, :, at]) for e in range(experts)])
        before = before + spread_bias(b1_v, at)
        hidden = (0.5 * before * (1.0 + lax.erf(before * math.sqrt(0.5)))).astype(BF16)
        return tuple(outs[e] + dot(hidden, w2_v[e, at, :]) for e in range(experts))

    outs = tuple(jnp.zeros((group, dim), F32) for _ in range(experts))
    outs = lax.fori_loop(0, ff // HIDDEN_CHUNK, expert_step, outs, unroll=True)
    result = (choose(outs) + spread_bias(b2_v, slice(None))).astype(BF16).astype(F32)
    even, odd = spread(result, rows)
    back_out[:, 0] = even.astype(BF16)
    back_out[:, 1] = odd.astype(BF16)

    def send_back(d):
        to, c, s = place(d)
        return pltpu.make_async_remote_copy(
            src_ref=back_out.at[c // 2, lax.rem(c, 2)],
            dst_ref=back_in.at[me // 2, lax.rem(me, 2)],
            send_sem=send_c.at[d],
            recv_sem=recv_c.at[me],
            device_id=(c, s),
            device_id_type=MESH,
        )

    def start_back(d, carry):
        send_back(d).start()
        return carry

    lax.fori_loop(1, devices, start_back, 0)
    back_in[me // 2, lax.rem(me, 2)] = back_out[c_me // 2, lax.rem(c_me, 2)]
    for copy in stats_sent:
        copy.wait_send()
    store.wait()

    def await_back(d, carry):
        origin, c, s = place(d)
        landed = back_in.at[origin // 2, lax.rem(origin, 2)]
        pltpu.make_async_copy(landed, landed, recv_c.at[origin]).wait()
        return carry

    lax.fori_loop(1, devices, await_back, 0)
    value = back_in[...].astype(F32)
    returned[...] = unspread(value[:, 0], value[:, 1], rows).astype(BF16)

    def finish(d, carry):
        send_sum(d).wait_send()
        send_back(d).wait_send()
        return carry

    lax.fori_loop(1, devices, finish, 0)


def mix(combine, returned, mixed):
    mixed[...] = dot(combine[...], returned[...]).astype(BF16)


def local(clips, shards, tokens, scales, slot_params, w1, b1, w2, b2):
    count, dim = tokens.shape[1:]
    blocks = scales.shape[1]
    slots = slot_params.shape[1]
    rows = slots // (clips * shards)
    devices = clips * shards
    piece = (2, 2 * rows, dim // 2)
    combine, returned = pl.pallas_call(
        functools.partial(kernel, clips, shards),
        out_shape=(
            jax.ShapeDtypeStruct((count, slots), BF16),
            jax.ShapeDtypeStruct((slots, dim), BF16),
        ),
        in_specs=[pl.BlockSpec(memory_space=pl.ANY)] * 7,
        out_specs=(pl.BlockSpec(memory_space=pl.ANY), pl.BlockSpec(memory_space=pltpu.VMEM)),
        scratch_shapes=[
            pltpu.VMEM((count, dim), BF16),
            pltpu.VMEM((blocks, 1, count), F32),
            pltpu.VMEM(slot_params.shape, BF16),
            pltpu.VMEM(w1.shape, BF16),
            pltpu.VMEM(b1.shape, BF16),
            pltpu.VMEM(w2.shape, BF16),
            pltpu.VMEM(b2.shape, BF16),
            pltpu.VMEM((count, slots), F32),
            pltpu.VMEM((count, slots), F32),
            pltpu.VMEM((count, slots), BF16),
            pltpu.VMEM((shards, 8, slots), F32),
            pltpu.VMEM((slots, dim), F32),
            pltpu.VMEM((devices // 2,) + piece, F32),
            pltpu.VMEM((shards, clips // 2) + piece, F32),
            pltpu.VMEM((clips // 2,) + piece, BF16),
            pltpu.VMEM((devices // 2,) + piece, BF16),
            pltpu.SemaphoreType.DMA((7,)),
            pltpu.SemaphoreType.DMA((count // CHUNK,)),
            pltpu.SemaphoreType.DMA((shards,)),
            pltpu.SemaphoreType.DMA((shards,)),
            pltpu.SemaphoreType.DMA((devices,)),
            pltpu.SemaphoreType.DMA((devices,)),
            pltpu.SemaphoreType.DMA((devices,)),
            pltpu.SemaphoreType.DMA((devices,)),
        ],
        compiler_params=pltpu.CompilerParams(
            collective_id=0, has_side_effects=True, vmem_limit_bytes=56 << 20
        ),
        name="slots",
    )(tokens[0], scales.transpose(1, 0, 2), slot_params, w1, b1, w2, b2)
    mixed = pl.pallas_call(
        mix,
        grid=(count // MIX_ROWS,),
        out_shape=jax.ShapeDtypeStruct((count, dim), BF16),
        in_specs=[
            pl.BlockSpec((MIX_ROWS, slots), lambda i: (i, 0)),
            pl.BlockSpec((slots, dim), lambda i: (0, 0)),
        ],
        out_specs=pl.BlockSpec((MIX_ROWS, dim), lambda i: (i, 0)),
        name="mix",
    )(combine, returned)
    return mixed[None]


def solution(mesh):
    placed = (
        P("clip", "shard", None),
        P("clip", None, "shard"),
        P(),
        P(("clip", "shard"), None, None),
        P(("clip", "shard"), None),
        P(("clip", "shard"), None, None),
        P(("clip", "shard"), None),
    )
    return jax.shard_map(
        functools.partial(local, mesh.shape["clip"], mesh.shape["shard"]),
        mesh=mesh,
        in_specs=placed,
        out_specs=P("clip", "shard", None),
        check_vma=False,
    )
```

time: 50.1 us -> 46 us (0.918)
  matrix products: 3.97 us -> 0 us
  local copies, waits for them, and re-layouts: 1.45 us -> 0 us
  Pallas kernels: 44.5 us -> 45.7 us
    pallas_call x0 -> x1, Pallas kernels: none -> 5.52 us  [local(): pl.pallas_call(mix, grid=(count // MIX_ROWS,), out_shape=jax.ShapeDtypeSt...]
    pallas_call x1, Pallas kernels: 44.5 us -> 40.2 us  [local(): pl.pallas_call(functools.partial(kernel, clips, shards), out_shape=(jax.S...]
    dot_general x1 -> x0, matrix products: 3.97 us -> none  [local(): mixed = jnp.dot(combine, returned, preferred_element_type=F32).astype(BF16)]
    unnamed x1 -> x0, local copies, waits for them, and re-layouts: 1.45 us -> none
where the time goes in v2:
time: 46 us; the launch traced here: 45.7 us
  Pallas kernels  45.7 us (99%)
    pallas_call x1, Pallas kernels, local(): pl.pallas_call(functools.partial(kernel, clips, shards), out_shape=(jax.S...  40.2 us
    pallas_call x1, Pallas kernels, local(): pl.pallas_call(mix, grid=(count // MIX_ROWS,), out_shape=jax.ShapeDtypeSt...  5.52 us

profile of v2, /device:TPU:0, one launch (start us, length us, event | category | flops | bytes accessed | tf_op | source)
XLA Modules:
  0.0 45.7 jit_solution(6650286132365245545)
XLA Ops:
  0.0 40.2 %slots.1 = (bf16[2304,128]{1,0:T(8,128)(2,1)}, bf16[128,768]{1,0:T(8,128)(2,1)}) custom-call(bf16[2304,768]{1,0:T(8,128)(2,1)} %bitcast.3, f32[6,1,2304]{2,1,0:T(1,128)} %bitcast.4, bf16[768,128]{1,0:T(8,128)(2,1)} %slot_params.1, bf16[2,768,3072]{2,1,0:T(8,128)(2,1)} %w1.1, bf16[2,3072]{1,0:T(2,128)(2,1)} %b1.1, bf16[2,3072,768]{2,1,0:T(8,128)(2,1)} %w2.1, ...), custom_call_target="tpu_custom_call" | custom-call | tf_op jit(solution)/shard_map/slots/pallas_call | solution.py:324
  40.2 5.5 %mix.1 = bf16[2304,768]{1,0:T(8,128)(2,1)} custom-call(bf16[2304,128]{1,0:T(8,128)(2,1)} %get-tuple-element.7.combine, bf16[128,768]{1,0:T(8,128)(2,1)} %get-tuple-element.8.returned), custom_call_target="tpu_custom_call" | custom-call | tf_op jit(solution)/shard_map/mix/pallas_call | solution.py:363

commit v3 on v2

--- a/solution.py
+++ b/solution.py
@@ -13,7 +13,6 @@
 MESH = pl.DeviceIdType.MESH
 CHUNK = 256
 HIDDEN_CHUNK = 768
-MIX_ROWS = 384
 
 
 def dot(a, b, contract=((1,), (0,))):
@@ -69,8 +68,8 @@
     logits,
     lifted,
     combine_v,
+    stats_out,
     stats,
-    partial,
     partial_out,
     sums,
     back_out,
@@ -98,7 +97,7 @@
     chunks = count // CHUNK
 
     def span(i):
-        return pl.ds(pl.multiple_of(i * CHUNK, CHUNK), CHUNK)
+        return pl.ds(i * CHUNK, CHUNK)
 
     load_scale = pltpu.make_async_copy(scales, scale_v, local_sem.at[0])
     load_params = pltpu.make_async_copy(slot_params, params_v, local_sem.at[1])
@@ -132,70 +131,53 @@
     load_params.wait()
     load_scale.wait()
 
-    def logits_step(i, peak):
+    peak = jnp.full((1, slots), -jnp.inf, F32)
+    for i in range(chunks):
         at = span(i)
         pltpu.make_async_copy(tokens.at[at], feat.at[at], token_sem.at[i]).wait()
         scale = scale_v[:, 0, at].T
-        for b in range(blocks):
-            lanes = slice(b * width, (b + 1) * width)
-            feat[at, lanes] = (feat[at, lanes].astype(F32) * scale[:, b : b + 1]).astype(BF16)
-        value = dot(feat[at, :], params_v[...])
+        scaled = jnp.concatenate(
+            [
+                feat[at, b * width : (b + 1) * width].astype(F32) * scale[:, b : b + 1]
+                for b in range(blocks)
+            ],
+            axis=1,
+        ).astype(BF16)
+        feat[at, :] = scaled
+        value = dot(scaled, params_v[...])
         logits[at, :] = value
-        return jnp.maximum(peak, jnp.max(value, axis=0, keepdims=True))
-
-    peak = lax.fori_loop(0, chunks, logits_step, jnp.full((1, slots), -jnp.inf, F32))
-
-    def sum_step(i, total):
+        peak = jnp.maximum(peak, jnp.max(value, axis=0, keepdims=True))
+
+    total = jnp.zeros((1, slots), F32)
+    for i in range(chunks):
         at = span(i)
         value = jnp.exp(logits[at, :] - peak)
-        lifted[at, :] = value
-        return total + jnp.sum(value, axis=0, keepdims=True)
-
-    total = lax.fori_loop(0, chunks, sum_step, jnp.zeros((1, slots), F32))
-    which = iota((8, slots), 0)
-    stats[s_me] = jnp.where(which == 0, peak, total)
+        total = total + jnp.sum(value, axis=0, keepdims=True)
+        high = value.astype(BF16)
+        low = (value - high.astype(F32)).astype(BF16)
+        lifted[at, :slots] = high
+        lifted[at, slots:] = low
+    stats_out[0:1, :] = peak
+    stats_out[1:2, :] = total
+    stats[me] = stats_out[...]
+    partial = dot(lifted[...], feat[...], ((0,), (0,)))
+    partial = partial[:slots] + partial[slots:]
+    even, odd = spread(partial, rows)
+    partial_out[:, 0] = even
+    partial_out[:, 1] = odd
 
     pl.semaphore_wait(barrier, devices - 1)
 
-    def shard_copies(make):
-        return [make(d, lax.rem(s_me + d, shards)) for d in range(1, shards)]
-
-    stats_sent = shard_copies(
-        lambda d, to: pltpu.make_async_remote_copy(
-            src_ref=stats.at[s_me],
-            dst_ref=stats.at[s_me],
+    def send_stats(d):
+        _, c, s = place(d)
+        return pltpu.make_async_remote_copy(
+            src_ref=stats_out,
+            dst_ref=stats.at[me],
             send_sem=send_a.at[d],
-            recv_sem=recv_a.at[s_me],
-            device_id=(c_me, to),
+            recv_sem=recv_a.at[me],
+            device_id=(c, s),
             device_id_type=MESH,
         )
-    )
-    for copy in stats_sent:
-        copy.start()
-
-    for d in range(1, shards):
-        origin = lax.rem(s_me + d, shards)
-        pltpu.make_async_copy(stats.at[origin], stats.at[origin], recv_a.at[origin]).wait()
-    top = stats[0, 0:1, :]
-    for s in range(1, shards):
-        top = jnp.maximum(top, stats[s, 0:1, :])
-    total = jnp.zeros((1, slots), F32)
-    for s in range(shards):
-        total = total + stats[s, 1:2, :] * jnp.exp(stats[s, 0:1, :] - top)
-
-    lift = jnp.exp(peak - top) / total
-    partial[...] = jnp.zeros(partial.shape, F32)
-
-    def partial_step(i, carry):
-        at = span(i)
-        dispatch = (lifted[at, :] * lift).astype(BF16)
-        partial[...] += dot(dispatch, feat[at, :], ((0,), (0,)))
-        return carry
-
-    lax.fori_loop(0, chunks, partial_step, 0)
-    even, odd = spread(partial[...], rows)
-    partial_out[:, 0] = even
-    partial_out[:, 1] = odd
 
     def send_sum(d):
         to, c, s = place(d)
@@ -210,19 +192,17 @@
 
     def start_sum(d, carry):
         send_sum(d).start()
+        send_stats(d).start()
         return carry
 
     lax.fori_loop(1, devices, start_sum, 0)
     sums[s_me, c_me // 2, lax.rem(c_me, 2)] = partial_out[me // 2, lax.rem(me, 2)]
 
-    def combine_step(i, carry):
+    for i in range(chunks):
         at = span(i)
         value = logits[at, :]
         weights = jnp.exp(value - jnp.max(value, axis=1, keepdims=True))
         combine_v[at, :] = (weights / jnp.sum(weights, axis=1, keepdims=True)).astype(BF16)
-        return carry
-
-    lax.fori_loop(0, chunks, combine_step, 0)
     store = pltpu.make_async_copy(combine_v, combine, local_sem.at[6])
     store.start()
 
@@ -230,13 +210,25 @@
         origin, c, s = place(d)
         landed = sums.at[s, c // 2, lax.rem(c, 2)]
         pltpu.make_async_copy(landed, landed, recv_b.at[origin]).wait()
+        pltpu.make_async_copy(stats.at[origin], stats.at[origin], recv_a.at[origin]).wait()
         return carry
 
     lax.fori_loop(1, devices, await_sum, 0)
-    value = sums[0]
-    for s in range(1, shards):
-        value = value + sums[s]
-    wide = unspread(value[:, 0], value[:, 1], rows).astype(BF16).astype(F32)
+    lane = iota((2 * rows, slots), 1) == me * rows + iota((2 * rows, slots), 0) % rows
+    share = stats[...].reshape(clips, shards, 2, slots)
+    weighted = []
+    for c in range(clips):
+        peaks = [share[c, s, 0:1] for s in range(shards)]
+        top = functools.reduce(jnp.maximum, peaks)
+        lifts = [jnp.exp(peaks[s] - top) for s in range(shards)]
+        total = sum(share[c, s, 1:2] * lifts[s] for s in range(shards))
+        value = jnp.zeros(sums.shape[3:], F32)
+        for s in range(shards):
+            own = jnp.sum(jnp.where(lane, lifts[s] / total, 0.0), axis=1, keepdims=True)
+            value = value + sums[s, c // 2, c % 2] * own
+        weighted.append(value[None])
+    even, odd = (jnp.concatenate(weighted[p::2], axis=0) for p in range(2))
+    wide = unspread(even, odd, rows).astype(BF16).astype(F32)
 
     mean = jnp.mean(wide * wide, axis=-1, keepdims=True)
     normalized = (wide * lax.rsqrt(mean + 1e-06)).astype(BF16)
@@ -288,8 +280,6 @@
 
     lax.fori_loop(1, devices, start_back, 0)
     back_in[me // 2, lax.rem(me, 2)] = back_out[c_me // 2, lax.rem(c_me, 2)]
-    for copy in stats_sent:
-        copy.wait_send()
     store.wait()
 
     def await_back(d, carry):
@@ -303,15 +293,12 @@
     returned[...] = unspread(value[:, 0], value[:, 1], rows).astype(BF16)
 
     def finish(d, carry):
+        send_stats(d).wait_send()
         send_sum(d).wait_send()
         send_back(d).wait_send()
         return carry
 
     lax.fori_loop(1, devices, finish, 0)
-
-
-def mix(combine, returned, mixed):
-    mixed[...] = dot(combine[...], returned[...]).astype(BF16)
 
 
 def local(clips, shards, tokens, scales, slot_params, w1, b1, w2, b2):
@@ -338,18 +325,18 @@
             pltpu.VMEM(w2.shape, BF16),
             pltpu.VMEM(b2.shape, BF16),
             pltpu.VMEM((count, slots), F32),
-            pltpu.VMEM((count, slots), F32),
+            pltpu.VMEM((count, 2 * slots), BF16),
             pltpu.VMEM((count, slots), BF16),
-            pltpu.VMEM((shards, 8, slots), F32),
-            pltpu.VMEM((slots, dim), F32),
+            pltpu.VMEM((2, slots), F32),
+            pltpu.VMEM((devices, 2, slots), F32),
             pltpu.VMEM((devices // 2,) + piece, F32),
             pltpu.VMEM((shards, clips // 2) + piece, F32),
             pltpu.VMEM((clips // 2,) + piece, BF16),
             pltpu.VMEM((devices // 2,) + piece, BF16),
             pltpu.SemaphoreType.DMA((7,)),
             pltpu.SemaphoreType.DMA((count // CHUNK,)),
-            pltpu.SemaphoreType.DMA((shards,)),
-            pltpu.SemaphoreType.DMA((shards,)),
+            pltpu.SemaphoreType.DMA((devices,)),
+            pltpu.SemaphoreType.DMA((devices,)),
             pltpu.SemaphoreType.DMA((devices,)),
             pltpu.SemaphoreType.DMA((devices,)),
             pltpu.SemaphoreType.DMA((devices,)),
@@ -360,17 +347,7 @@
         ),
         name="slots",
     )(tokens[0], scales.transpose(1, 0, 2), slot_params, w1, b1, w2, b2)
-    mixed = pl.pallas_call(
-        mix,
-        grid=(count // MIX_ROWS,),
-        out_shape=jax.ShapeDtypeStruct((count, dim), BF16),
-        in_specs=[
-            pl.BlockSpec((MIX_ROWS, slots), lambda i: (i, 0)),
-            pl.BlockSpec((slots, dim), lambda i: (0, 0)),
-        ],
-        out_specs=pl.BlockSpec((MIX_ROWS, dim), lambda i: (i, 0)),
-        name="mix",
-    )(combine, returned)
+    mixed = jnp.dot(combine, returned, preferred_element_type=F32).astype(BF16)
     return mixed[None]
 
 

time: 46 us -> 41.2 us (0.90)
  Pallas kernels: 45.7 us -> 37.1 us
  matrix products: 0 us -> 3.96 us
    pallas_call x1 -> x0, Pallas kernels: 5.52 us -> none  [local(): pl.pallas_call(mix, grid=(count // MIX_ROWS,), out_shape=jax.ShapeDtypeSt...]
    dot_general x0 -> x1, matrix products: none -> 3.96 us  [local(): mixed = jnp.dot(combine, returned, preferred_element_type=F32).astype(BF16)]
    pallas_call x1, Pallas kernels: 40.2 us -> 37.1 us  [local(): pl.pallas_call(functools.partial(kernel, clips, shards), out_shape=(jax.S...]
where the time goes in v3:
time: 41.2 us; the launch traced here: 41.1 us
  Pallas kernels  37.1 us (90%)
  matrix products  3.96 us (10%)
    pallas_call x1, Pallas kernels, local(): pl.pallas_call(functools.partial(kernel, clips, shards), out_shape=(jax.S...  37.1 us
    dot_general x1, matrix products, local(): mixed = jnp.dot(combine, returned, preferred_element_type=F32).astype(BF16)  3.96 us

profile of v3, /device:TPU:0, one launch (start us, length us, event | category | flops | bytes accessed | tf_op | source)
XLA Modules:
  0.0 41.1 jit_solution(4935690636702780673)
XLA Ops:
  0.0 37.1 %slots.1 = (bf16[2304,128]{1,0:T(8,128)(2,1)}, bf16[128,768]{1,0:T(8,128)(2,1)}) custom-call(bf16[2304,768]{1,0:T(8,128)(2,1)} %bitcast.6, f32[6,1,2304]{2,1,0:T(1,128)} %bitcast.7, bf16[768,128]{1,0:T(8,128)(2,1)} %slot_params.1, bf16[2,768,3072]{2,1,0:T(8,128)(2,1)} %w1.1, bf16[2,3072]{1,0:T(2,128)(2,1)} %b1.1, bf16[2,3072,768]{2,1,0:T(8,128)(2,1)} %w2.1, ...), custom_call_target="tpu_custom_call" | custom-call | tf_op jit(solution)/shard_map/slots/pallas_call | solution.py:311
  37.1 4.0 %fusion = bf16[1,2304,768]{2,1,0:T(8,128)(2,1)} fusion(bf16[2304,128]{1,0:T(8,128)(2,1)} %get-tuple-element.7, bf16[128,768]{1,0:T(8,128)(2,1)} %get-tuple-element.8), kind=kOutput, calls=%fused_computation.1 | convolution fusion | flops 454754304 | bytes 4325376 | tf_op jit(solution)/shard_map/dot_general | solution.py:350

commit v4 on v2

--- a/solution.py
+++ b/solution.py
@@ -13,7 +13,6 @@
 MESH = pl.DeviceIdType.MESH
 CHUNK = 256
 HIDDEN_CHUNK = 768
-MIX_ROWS = 384
 
 
 def dot(a, b, contract=((1,), (0,))):
@@ -70,7 +69,7 @@
     lifted,
     combine_v,
     stats,
-    partial,
+    lifted_v,
     partial_out,
     sums,
     back_out,
@@ -98,7 +97,7 @@
     chunks = count // CHUNK
 
     def span(i):
-        return pl.ds(pl.multiple_of(i * CHUNK, CHUNK), CHUNK)
+        return pl.ds(i * CHUNK, CHUNK)
 
     load_scale = pltpu.make_async_copy(scales, scale_v, local_sem.at[0])
     load_params = pltpu.make_async_copy(slot_params, params_v, local_sem.at[1])
@@ -132,26 +131,29 @@
     load_params.wait()
     load_scale.wait()
 
-    def logits_step(i, peak):
+    peak = jnp.full((1, slots), -jnp.inf, F32)
+    for i in range(chunks):
         at = span(i)
         pltpu.make_async_copy(tokens.at[at], feat.at[at], token_sem.at[i]).wait()
         scale = scale_v[:, 0, at].T
-        for b in range(blocks):
-            lanes = slice(b * width, (b + 1) * width)
-            feat[at, lanes] = (feat[at, lanes].astype(F32) * scale[:, b : b + 1]).astype(BF16)
-        value = dot(feat[at, :], params_v[...])
+        scaled = jnp.concatenate(
+            [
+                feat[at, b * width : (b + 1) * width].astype(F32) * scale[:, b : b + 1]
+                for b in range(blocks)
+            ],
+            axis=1,
+        ).astype(BF16)
+        feat[at, :] = scaled
+        value = dot(scaled, params_v[...])
         logits[at, :] = value
-        return jnp.maximum(peak, jnp.max(value, axis=0, keepdims=True))
-
-    peak = lax.fori_loop(0, chunks, logits_step, jnp.full((1, slots), -jnp.inf, F32))
-
-    def sum_step(i, total):
+        peak = jnp.maximum(peak, jnp.max(value, axis=0, keepdims=True))
+
+    total = jnp.zeros((1, slots), F32)
+    for i in range(chunks):
         at = span(i)
         value = jnp.exp(logits[at, :] - peak)
         lifted[at, :] = value
-        return total + jnp.sum(value, axis=0, keepdims=True)
-
-    total = lax.fori_loop(0, chunks, sum_step, jnp.zeros((1, slots), F32))
+        total = total + jnp.sum(value, axis=0, keepdims=True)
     which = iota((8, slots), 0)
     stats[s_me] = jnp.where(which == 0, peak, total)
 
@@ -184,16 +186,11 @@
         total = total + stats[s, 1:2, :] * jnp.exp(stats[s, 0:1, :] - top)
 
     lift = jnp.exp(peak - top) / total
-    partial[...] = jnp.zeros(partial.shape, F32)
-
-    def partial_step(i, carry):
+    for i in range(chunks):
         at = span(i)
-        dispatch = (lifted[at, :] * lift).astype(BF16)
-        partial[...] += dot(dispatch, feat[at, :], ((0,), (0,)))
-        return carry
-
-    lax.fori_loop(0, chunks, partial_step, 0)
-    even, odd = spread(partial[...], rows)
+        lifted_v[at, :] = (lifted[at, :] * lift).astype(BF16)
+    partial = dot(lifted_v[...], feat[...], ((0,), (0,)))
+    even, odd = spread(partial, rows)
     partial_out[:, 0] = even
     partial_out[:, 1] = odd
 
@@ -215,14 +212,11 @@
     lax.fori_loop(1, devices, start_sum, 0)
     sums[s_me, c_me // 2, lax.rem(c_me, 2)] = partial_out[me // 2, lax.rem(me, 2)]
 
-    def combine_step(i, carry):
+    for i in range(chunks):
         at = span(i)
         value = logits[at, :]
         weights = jnp.exp(value - jnp.max(value, axis=1, keepdims=True))
         combine_v[at, :] = (weights / jnp.sum(weights, axis=1, keepdims=True)).astype(BF16)
-        return carry
-
-    lax.fori_loop(0, chunks, combine_step, 0)
     store = pltpu.make_async_copy(combine_v, combine, local_sem.at[6])
     store.start()
 
@@ -308,10 +302,6 @@
         return carry
 
     lax.fori_loop(1, devices, finish, 0)
-
-
-def mix(combine, returned, mixed):
-    mixed[...] = dot(combine[...], returned[...]).astype(BF16)
 
 
 def local(clips, shards, tokens, scales, slot_params, w1, b1, w2, b2):
@@ -341,7 +331,7 @@
             pltpu.VMEM((count, slots), F32),
             pltpu.VMEM((count, slots), BF16),
             pltpu.VMEM((shards, 8, slots), F32),
-            pltpu.VMEM((slots, dim), F32),
+            pltpu.VMEM((count, slots), BF16),
             pltpu.VMEM((devices // 2,) + piece, F32),
             pltpu.VMEM((shards, clips // 2) + piece, F32),
             pltpu.VMEM((clips // 2,) + piece, BF16),
@@ -360,17 +350,7 @@
         ),
         name="slots",
     )(tokens[0], scales.transpose(1, 0, 2), slot_params, w1, b1, w2, b2)
-    mixed = pl.pallas_call(
-        mix,
-        grid=(count // MIX_ROWS,),
-        out_shape=jax.ShapeDtypeStruct((count, dim), BF16),
-        in_specs=[
-            pl.BlockSpec((MIX_ROWS, slots), lambda i: (i, 0)),
-            pl.BlockSpec((slots, dim), lambda i: (0, 0)),
-        ],
-        out_specs=pl.BlockSpec((MIX_ROWS, dim), lambda i: (i, 0)),
-        name="mix",
-    )(combine, returned)
+    mixed = jnp.dot(combine, returned, preferred_element_type=F32).astype(BF16)
     return mixed[None]
 
 

time: 46 us -> 42.5 us (0.924)
  Pallas kernels: 45.7 us -> 38.4 us
  matrix products: 0 us -> 3.97 us
    pallas_call x1 -> x0, Pallas kernels: 5.52 us -> none  [local(): pl.pallas_call(mix, grid=(count // MIX_ROWS,), out_shape=jax.ShapeDtypeSt...]
    dot_general x0 -> x1, matrix products: none -> 3.97 us  [local(): mixed = jnp.dot(combine, returned, preferred_element_type=F32).astype(BF16)]
    pallas_call x1, Pallas kernels: 40.2 us -> 38.4 us  [local(): pl.pallas_call(functools.partial(kernel, clips, shards), out_shape=(jax.S...]
where the time goes in v4:
time: 42.5 us; the launch traced here: 42.4 us
  Pallas kernels  38.4 us (90%)
  matrix products  3.97 us (9%)
    pallas_call x1, Pallas kernels, local(): pl.pallas_call(functools.partial(kernel, clips, shards), out_shape=(jax.S...  38.4 us
    dot_general x1, matrix products, local(): mixed = jnp.dot(combine, returned, preferred_element_type=F32).astype(BF16)  3.97 us

profile of v4, /device:TPU:0, one launch (start us, length us, event | category | flops | bytes accessed | tf_op | source)
XLA Modules:
  0.0 42.4 jit_solution(4357668734376879594)
XLA Ops:
  0.0 38.4 %slots.1 = (bf16[2304,128]{1,0:T(8,128)(2,1)}, bf16[128,768]{1,0:T(8,128)(2,1)}) custom-call(bf16[2304,768]{1,0:T(8,128)(2,1)} %bitcast.6, f32[6,1,2304]{2,1,0:T(1,128)} %bitcast.7, bf16[768,128]{1,0:T(8,128)(2,1)} %slot_params.1, bf16[2,768,3072]{2,1,0:T(8,128)(2,1)} %w1.1, bf16[2,3072]{1,0:T(2,128)(2,1)} %b1.1, bf16[2,3072,768]{2,1,0:T(8,128)(2,1)} %w2.1, ...), custom_call_target="tpu_custom_call" | custom-call | tf_op jit(solution)/shard_map/slots/pallas_call | solution.py:314
  38.4 4.0 %fusion = bf16[1,2304,768]{2,1,0:T(8,128)(2,1)} fusion(bf16[2304,128]{1,0:T(8,128)(2,1)} %get-tuple-element.7, bf16[128,768]{1,0:T(8,128)(2,1)} %get-tuple-element.8), kind=kOutput, calls=%fused_computation.1 | convolution fusion | flops 454754304 | bytes 4325376 | tf_op jit(solution)/shard_map/dot_general | solution.py:353
